TPU v7x, 32 devices: a whole 2x2x4 slice. The times are simulated.
32 devices in a mesh: row: 4 (over z), col: 2 (over x), depth: 4 (over y, core).
Axes of the slice: x: 2, y: 2, z: 4, core: 2. Of those that a mesh axis runs over, the one named last changes fastest.
Arguments:
- amplitudes: bfloat16 [3200, 7200], P('row', ('col', 'depth')), may hold values from -6 to 6
- integrals: bfloat16 [7200, 4096], P('row', ('col', 'depth')), may hold values from -0.0625 to 0.0625
- cycle_integrals: bfloat16 [256, 256], P('row'), as said below
- occ_irrep: int32 [100], replicated, may hold values from 0 to 7
- vir_irrep: int32 [900], replicated, may hold values from 0 to 7
Outputs:
- ladder: bfloat16 [3200, 4096], P('row', ('col', 'depth'))
- cycle: bfloat16 [256, 57600], P('row', ('col', 'depth'))
Inputs may be any that keep to these rules, and one draw needn't show every extreme that they name: cycle_integrals equals its transpose.
All inputs are finite; a program needn't handle non-finite values.
Results may differ from a plain program's by a relative error of at most 0.001.
Values may be sent and summed in bfloat16 or wider, within the bound.
A program may use at most 128 MiB of HBM per device.

v0:
```python
import jax
import jax.numpy as jnp
from jax import lax
from jax.sharding import PartitionSpec as P

NO = 100
NV = 900
JW = 64
CW = 8


def label_bits(labels):
    return jnp.stack([labels % 2, labels // 2 % 2, labels // 4 % 2])


def lookup(lookup_table, indices):
    matches = indices[:, None] == jnp.arange(lookup_table.shape[0], dtype=jnp.int32)[None, :]
    return jnp.sum(jnp.where(matches, lookup_table[None, :], 0), axis=1)


def shards(amplitudes, integrals, cycle_integrals, occ_irrep, vir_irrep):
    rows_here = amplitudes.shape[0]
    occ_block = rows_here // NO
    local_cols = amplitudes.shape[1]
    regroup_in = amplitudes.reshape(occ_block, NO, local_cols)[:, :JW, :]
    spread = lax.all_to_all(regroup_in, ("col", "depth"), split_axis=1, concat_axis=2, tiled=True)
    occ_here = spread.shape[1]
    ordered = (
        spread.reshape(occ_block, occ_here, CW, NV)
        .transpose(0, 2, 1, 3)
        .reshape(occ_block * CW, occ_here * NV)
    )
    columns = occ_here * NV
    integ_all = lax.all_gather(integrals, "row", axis=0, tiled=True)
    ladder_sum = jnp.dot(
        lax.all_gather(amplitudes, ("col", "depth"), axis=1, tiled=True),
        integ_all,
        preferred_element_type=jnp.float32,
    )
    ladder = ladder_sum.astype(jnp.bfloat16)
    cycle_rows_here = cycle_integrals.shape[0]
    cycle_sum = lax.psum_scatter(
        lax.dot_general(
            cycle_integrals, ordered, (((0,), (0,)), ((), ())), preferred_element_type=jnp.float32
        ),
        "row",
        scatter_dimension=0,
        tiled=True,
    )
    occ_bits = label_bits(occ_irrep)
    vir_bits = label_bits(vir_irrep)
    row_ids = lax.axis_index("row") * cycle_rows_here + jnp.arange(cycle_rows_here, dtype=jnp.int32)
    column_ids = lax.axis_index(("col", "depth")) * columns + jnp.arange(columns, dtype=jnp.int32)
    occ_first = row_ids // CW
    virt_first = row_ids % CW
    occ_second = column_ids // NV
    virt_second = column_ids % NV
    odd_count = jnp.zeros((cycle_rows_here, columns), jnp.int32)
    for digit in range(3):
        row_bits = lookup(occ_bits[digit], occ_first) + lookup(vir_bits[digit], virt_first)
        column_bits = lookup(occ_bits[digit], occ_second) + lookup(vir_bits[digit], virt_second)
        odd_count = odd_count + (row_bits[:, None] + column_bits[None, :]) % 2
    cycle = jnp.where(odd_count == 0, cycle_sum, jnp.float32(0.0)).astype(jnp.bfloat16)
    return (ladder, cycle)


def solution(mesh):
    in_specs = (P("row", ("col", "depth")), P("row", ("col", "depth")), P("row", None), P(), P())
    out_specs = (P("row", ("col", "depth")), P("row", ("col", "depth")))
    return jax.shard_map(shards, mesh=mesh, in_specs=in_specs, out_specs=out_specs, check_vma=False)
```

profile of v0, /device:TPU:0, one launch (start us, length us, event | category | flops | bytes accessed | tf_op | source)
XLA Modules:
  0.0 310.4 jit_solution(11669424504243657550)
XLA Ops:
  8.0 0.0 copy-start
  8.0 0.0 reduce-scatter.2.cloned.1.call-start
  8.1 3.8 %reshape.104 = bf16[8,100,900]{1,0,2:T(8,128)(2,1)S(1)} reshape(bf16[800,900]{0,1:T(8,128)(2,1)} %param.5) | data formatting | bytes 2880000 | tf_op jit(solution)/shard_map/reshape | solution.py:25
  11.8 2.8 copy.15
  14.7 19.6 %all_to_all.4 = bf16[8,64,900]{2,0,1:T(8,128)(2,1)S(1)} all-to-all(bf16[8,64,900]{2,0,1:T(8,128)(2,1)S(1)} %copy.15), channel_id=1, replica_groups=mesh['row'=4,'col'=2,'depth'=4] {'col','depth'}, dimensions={1} | all-to-all | bytes 1843200 | tf_op jit(solution)/shard_map/all_to_all | solution.py:26
  34.3 0.6 copy.16
  34.9 1.3 reshape.100
  36.2 0.0 copy-done
  36.2 4.2 %fusion.18 = f32[256,7200]{1,0:T(8,128)} fusion(bf16[64,256]{1,0:T(8,128)(2,1)S(1)} %copy-done, bf16[64,7200]{1,0:T(8,128)(2,1)S(1)} %reshape.100), kind=kOutput, calls=%fused_computation.91 | convolution fusion | flops 235929600 | bytes 8327168 | tf_op jit(solution)/shard_map/dot_general | solution.py:43
  40.4 0.0 reduce-scatter.2.cloned.1.call-update
  40.4 0.0 copy-start.2
  40.4 0.0 copy-start.1
  40.5 0.0 all-gather.6.cloned.1.call-start
  40.5 0.5 all-gather.6.cloned.1.call-update
  41.0 0.2 all-gather.4.cloned.1.call-start
  41.3 0.4 all-gather.4.cloned.1.call-update
  41.7 0.0 copy-done.2
  41.7 0.0 copy-done.1
  41.7 1.1 select_reduce_fusion.5
  42.9 9.3 %select_reduce_fusion.2 = (s32[7200]{0:T(1024)S(1)}, s32[7200]{0:T(1024)S(1)}, s32[7200]{0:T(1024)S(1)}) fusion(s32[900]{0:T(1024)S(1)} %get-tuple-element.16, s32[7200]{0:T(1024)S(1)} %get-tuple-element.20, s32[900]{0:T(1024)S(1)} %get-tuple-element.15, s32[900]{0:T(1024)S(1)} %get-tuple-element.14), kind=kLoop, calls=%fused_computation.2 | loop fusion | flops 45338400 | bytes 126000 | tf_op jit(solution)/shard_map/reduce_sum | solution.py:18
  52.2 0.2 select_reduce_fusion.11
  52.4 0.3 select_reduce_fusion.8
  52.8 157.8 %reduce-scatter.2.cloned.1.call-done = f32[64,7200]{1,0:T(8,128)} async-done(((f32[256,7200]{1,0:T(8,128)}), f32[64,7200]{1,0:T(8,128)}) %reduce-scatter.2.cloned.1.call-update) | async-done | bytes 1843216 | tf_op jit(solution)/shard_map/reduce_scatter | solution.py:42
  210.5 4.6 %select_convert_fusion = bf16[64,7200]{1,0:T(8,128)(2,1)} fusion(f32[64,7200]{1,0:T(8,128)} %reduce-scatter.2.cloned.1.call-done, s32[7200]{0:T(1024)S(1)} %add.222, s32[64]{0:T(128)S(1)} %add.220, s32[7200]{0:T(1024)S(1)} %add.213, s32[64]{0:T(128)S(1)} %add.211, s32[7200]{0:T(1024)S(1)} %add.205, s32[64]{0:T(128)S(1)} %add.199), kind=kLoop, calls=%fused_computation.29 | loop fusion | flops 18432000 | bytes 2851968 | tf_op jit(solution)/shard_map/convert_element_type | solution.py:63
  215.1 0.0 all-gather.6.cloned.1.call-done
  215.1 12.2 %reshape.103 = bf16[7200,800]{1,0:T(8,128)(2,1)} reshape(bf16[8,900,800]{2,1,0:T(8,128)(2,1)} %all-gather.6.cloned.1.call-done) | data formatting | bytes 23040000
  227.3 61.8 %all-gather.4.cloned.1.call-done = bf16[7200,512]{1,0:T(8,128)(2,1)} async-done(((bf16[1800,512]{1,0:T(8,128)(2,1)}), bf16[7200,512]{1,0:T(8,128)(2,1)}) %all-gather.4.cloned.1.call-update) | async-done | bytes 7372816 | tf_op jit(solution)/shard_map/all_gather | solution.py:34
  289.1 13.9 %convolution_convert_fusion = bf16[800,512]{1,0:T(8,128)(2,1)} fusion(bf16[7200,800]{1,0:T(8,128)(2,1)} %reshape.103, bf16[7200,512]{1,0:T(8,128)(2,1)} %all-gather.4.cloned.1.call-done), kind=kOutput, calls=%fused_computation.30 | convolution fusion | flops 5898649600 | bytes 19712000 | tf_op jit(solution)/shard_map/dot_general | solution.py:35
  (10 shorter events, 0.1 us)
Async XLA Ops:
  8.0 28.2 %copy-start = (bf16[64,256]{1,0:T(8,128)(2,1)S(1)}, bf16[64,256]{1,0:T(8,128)(2,1)}, u32[]{:S(2)}) copy-start(bf16[64,256]{1,0:T(8,128)(2,1)} %param.7) | copy-start | bytes 98308
  8.0 202.5 %reduce-scatter.2.cloned.1.call-start = ((), (), s32[]{:S(2)}) async-start(), calls=%async_computation.3 | async-start | bytes 9338880 | tf_op jit(solution)/shard_map/reduce_scatter | solution.py:42
  40.4 1.2 copy-start.2
  40.4 1.3 copy-start.1
  40.5 174.6 %all-gather.6.cloned.1.call-start = ((), (), s32[]{:S(2)}) async-start(), calls=%async_computation.4 | async-start | bytes 14579712 | tf_op jit(solution)/shard_map/all_gather | solution.py:36
  41.0 248.0 %all-gather.4.cloned.1.call-start = ((), (), s32[]{:S(2)}) async-start(), calls=%async_computation.2 | async-start | bytes 9216000 | tf_op jit(solution)/shard_map/all_gather | solution.py:34
Sparse Core Ops, SparseCore 0:
  40.5 169.9 reduce-scatter.1
Sparse Core Ops, SparseCore 1:
  42.8 73.7 all-gather.5
  118.0 171.0 all-gather.3
where the time goes:
time: 311 us; the launch traced here: 310 us
  waiting for transfers between devices  220 us (71%)
  local copies, waits for them, and re-layouts  20.7 us (7%)
  blocking collectives  19.6 us (6%)
  matrix products  18.1 us (6%)
  between operations  15.7 us (5%)
  other arithmetic  15.6 us (5%)
    reduce_scatter x1, waiting for transfers between devices, shards(): lax.psum_scatter(lax.dot_general(cycle_integrals, ordered, (((0,), (0,)),...  158 us
    all_gather x1, waiting for transfers between devices, shards(): integ_all = lax.all_gather(integrals, 'row', axis=0, tiled=True)  61.8 us
    all_to_all x1, blocking collectives, shards(): lax.all_to_all(regroup_in, ('col', 'depth'), split_axis=1, concat_axis=2,...  19.6 us
    dot_general x1, matrix products, shards(): jnp.dot(lax.all_gather(amplitudes, ('col', 'depth'), axis=1, tiled=True),...  13.9 us
    unnamed x7, local copies, waits for them, and re-layouts  12.2 us
    reduce_sum x4, other arithmetic, lookup(): return jnp.sum(jnp.where(matches, lookup_table[None, :], 0), axis=1)  10.9 us
  transfers between devices with their start and end apart: 3, of which 2 were waited for; matrix products, arithmetic and copies ran while one was open for 9% of the time, Pallas kernels for 0%

commit v1 on v0

--- a/solution.py
+++ b/solution.py
@@ -2,11 +2,28 @@
 import jax.numpy as jnp
 from jax import lax
 from jax.sharding import PartitionSpec as P
+from jax.lax import axis_index, axis_size, ppermute
 
 NO = 100
 NV = 900
 JW = 64
 CW = 8
+
+
+def direct_pieces_all(raw, axis_name, d0):
+    n_all = axis_size(axis_name)
+    crops = [(pp, (pp + 1) % n_all) for pp in range(n_all)]
+
+    def time_the_goods(x_new):
+        if len(x_new) == n_all:
+            return x_new
+        high = time_the_goods([ppermute(x_new[0], axis_name, crops), *x_new])
+        return high
+
+    z_new = jnp.roll(
+        jnp.concatenate(time_the_goods([raw]), d0), (axis_index(axis_name) + 1) * raw.shape[d0], d0
+    )
+    return z_new
 
 
 def label_bits(labels):
@@ -31,7 +48,7 @@
         .reshape(occ_block * CW, occ_here * NV)
     )
     columns = occ_here * NV
-    integ_all = lax.all_gather(integrals, "row", axis=0, tiled=True)
+    integ_all = direct_pieces_all(integrals, "row", 0)
     ladder_sum = jnp.dot(
         lax.all_gather(amplitudes, ("col", "depth"), axis=1, tiled=True),
         integ_all,

time: 311 us -> 343 us (1.10)
  starting transfers between devices: 0.3 us -> 37.8 us
  waiting for transfers between devices: 220 us -> 195 us
  local copies, waits for them, and re-layouts: 20.7 us -> 41.6 us
    ppermute x0 -> x3, waiting for transfers between devices: none -> 194 us  [time_the_goods(): high = time_the_goods([ppermute(x_new[0], axis_name, crops), *x_new])]
    reduce_scatter x1, waiting for transfers between devices: 158 us -> 0.01 us  [shards(): lax.psum_scatter(lax.dot_general(cycle_integrals, ordered, (((0,), (0,)),...]
    all_gather x1 -> x0, waiting for transfers between devices: 61.8 us -> none  [shards(): integ_all = lax.all_gather(integrals, 'row', axis=0, tiled=True)]
    ppermute x0 -> x3, starting transfers between devices: none -> 37.7 us  [time_the_goods(): high = time_the_goods([ppermute(x_new[0], axis_name, crops), *x_new])]
    unnamed x7 -> x16, local copies, waits for them, and re-layouts: 12.2 us -> 31.7 us
  transfers between devices with their start and end apart: 3 -> 5, of which waited for: 2 -> 3; matrix products, arithmetic and copies ran while one was open for 9% -> 10% of each run, Pallas kernels for 0% -> 0%
where the time goes in v1:
time: 343 us
  waiting for transfers between devices  195 us (57%)
  local copies, waits for them, and re-layouts  41.6 us (12%)
  starting transfers between devices  37.8 us (11%)
  blocking collectives  19.6 us (6%)
  matrix products  18 us (5%)
  other arithmetic  15.6 us (5%)
  between operations  15.6 us (5%)
    ppermute x3, waiting for transfers between devices, time_the_goods(): high = time_the_goods([ppermute(x_new[0], axis_name, crops), *x_new])  194 us
    ppermute x3, starting transfers between devices, time_the_goods(): high = time_the_goods([ppermute(x_new[0], axis_name, crops), *x_new])  37.7 us
    unnamed x16, local copies, waits for them, and re-layouts  31.7 us
    all_to_all x1, blocking collectives, shards(): lax.all_to_all(regroup_in, ('col', 'depth'), split_axis=1, concat_axis=2,...  19.6 us
    dot_general x1, matrix products, shards(): jnp.dot(lax.all_gather(amplitudes, ('col', 'depth'), axis=1, tiled=True),...  13.9 us
    reduce_sum x4, other arithmetic, lookup(): return jnp.sum(jnp.where(matches, lookup_table[None, :], 0), axis=1)  10.9 us
  transfers between devices with their start and end apart: 5, of which 3 were waited for; matrix products, arithmetic and copies ran while one was open for 10% of the time, Pallas kernels for 0%

profile of v1, /device:TPU:0, one launch (start us, length us, event | category | flops | bytes accessed | tf_op | source)
XLA Modules:
  0.0 343.0 jit_solution(14730393984190240144)
XLA Ops:
  8.0 0.0 reduce-scatter.2.cloned.1.call-start
  8.1 3.8 %reshape.104 = bf16[8,100,900]{1,0,2:T(8,128)(2,1)S(1)} reshape(bf16[800,900]{0,1:T(8,128)(2,1)} %param.5) | data formatting | bytes 2880000 | tf_op jit(solution)/shard_map/reshape | solution.py:42
  11.8 2.8 copy.15
  14.7 19.6 %all_to_all.4 = bf16[8,64,900]{2,0,1:T(8,128)(2,1)S(1)} all-to-all(bf16[8,64,900]{2,0,1:T(8,128)(2,1)S(1)} %copy.15), channel_id=1, replica_groups=mesh['row'=4,'col'=2,'depth'=4] {'col','depth'}, dimensions={1} | all-to-all | bytes 1843200 | tf_op jit(solution)/shard_map/all_to_all | solution.py:43
  34.3 0.6 copy.16
  34.9 1.3 reshape.100
  36.2 4.2 %fusion.27 = f32[256,7200]{1,0:T(8,128)} fusion(bf16[64,256]{1,0:T(8,128)(2,1)S(1)} %copy-done, bf16[64,7200]{1,0:T(8,128)(2,1)S(1)} %reshape.100), kind=kOutput, calls=%fused_computation.103 | convolution fusion | flops 235929600 | bytes 8327168 | tf_op jit(solution)/shard_map/dot_general | solution.py:60
  40.4 0.0 reduce-scatter.2.cloned.1.call-update
  40.4 0.0 all-gather.3.cloned.1.call-start
  40.4 0.5 all-gather.3.cloned.1.call-update
  41.0 0.9 copy-done.1
  41.9 1.6 collective-permute-start
  43.4 78.3 %collective-permute-done = bf16[1800,512]{1,0:T(8,128)(2,1)} collective-permute-done((bf16[1800,512]{1,0:T(8,128)(2,1)S(1)}, bf16[1800,512]{1,0:T(8,128)(2,1)}, u32[]{:S(2)}, u32[]{:S(2)}) %collective-permute-start) | collective-permute-done | bytes 1843232 | tf_op jit(solution)/shard_map/ppermute | solution.py:20
  121.8 34.9 %collective-permute-start.1 = (bf16[1800,512]{1,0:T(8,128)(2,1)}, bf16[1800,512]{1,0:T(8,128)(2,1)}, u32[]{:S(2)}, u32[]{:S(2)}) collective-permute-start(bf16[1800,512]{1,0:T(8,128)(2,1)} %collective-permute-done), channel_id=1, source_target_pairs={{0,8},{8,16},{16,24},{24,0},{1,9},{9,17},{17,25},{25,1},{2,10},{10... | collective-permute-start | bytes 5529608 | tf_op jit(solution)/shard_map/ppermute | solution.py:20
  156.8 1.1 select_reduce_fusion.5
  157.9 80.1 %collective-permute-done.1 = bf16[1800,512]{1,0:T(8,128)(2,1)} collective-permute-done((bf16[1800,512]{1,0:T(8,128)(2,1)}, bf16[1800,512]{1,0:T(8,128)(2,1)}, u32[]{:S(2)}, u32[]{:S(2)}) %collective-permute-start.1) | collective-permute-done | bytes 1843232 | tf_op jit(solution)/shard_map/ppermute | solution.py:20
  238.0 1.2 collective-permute-start.2
  239.2 9.3 %select_reduce_fusion.2 = (s32[7200]{0:T(1024)S(1)}, s32[7200]{0:T(1024)S(1)}, s32[7200]{0:T(1024)S(1)}) fusion(s32[900]{0:T(1024)S(1)} %get-tuple-element.16, s32[7200]{0:T(1024)S(1)} %get-tuple-element.20, s32[900]{0:T(1024)S(1)} %get-tuple-element.15, s32[900]{0:T(1024)S(1)} %get-tuple-element.14), kind=kLoop, calls=%fused_computation.2 | loop fusion | flops 45338400 | bytes 126000 | tf_op jit(solution)/shard_map/reduce_sum | solution.py:35
  248.6 0.2 select_reduce_fusion.11
  248.8 0.3 select_reduce_fusion.8
  249.1 35.8 %collective-permute-done.2 = bf16[1800,512]{1,0:T(8,128)(2,1)} collective-permute-done((bf16[1800,512]{1,0:T(8,128)(2,1)}, bf16[1800,512]{1,0:T(8,128)(2,1)}, u32[]{:S(2)}, u32[]{:S(2)}) %collective-permute-start.2) | collective-permute-done | bytes 1843232 | tf_op jit(solution)/shard_map/ppermute | solution.py:20
  284.9 2.9 constant_dynamic-update-slice_fusion.7
  287.8 2.8 constant_dynamic-update-slice_fusion.6
  290.6 2.9 constant_dynamic-update-slice_fusion.5
  293.5 1.4 constant_dynamic-update-slice_fusion.4
  294.9 2.9 constant_dynamic-update-slice_fusion.3
  297.8 2.9 constant_dynamic-update-slice_fusion.2
  300.7 2.9 constant_dynamic-update-slice_fusion.1
  303.5 1.4 constant_dynamic-update-slice_fusion
  304.9 4.6 %select_convert_fusion = bf16[64,7200]{1,0:T(8,128)(2,1)} fusion(f32[64,7200]{1,0:T(8,128)} %reduce-scatter.2.cloned.1.call-done, s32[7200]{0:T(1024)S(1)} %add.238, s32[64]{0:T(128)S(1)} %add.236, s32[7200]{0:T(1024)S(1)} %add.229, s32[64]{0:T(128)S(1)} %add.227, s32[7200]{0:T(1024)S(1)} %add.221, s32[64]{0:T(128)S(1)} %add.215), kind=kLoop, calls=%fused_computation.31 | loop fusion | flops 18432000 | bytes 2851968 | tf_op jit(solution)/shard_map/convert_element_type | solution.py:80
  309.5 12.2 %reshape.103 = bf16[7200,800]{1,0:T(8,128)(2,1)} reshape(bf16[8,900,800]{2,1,0:T(8,128)(2,1)} %all-gather.3.cloned.1.call-done) | data formatting | bytes 23040000
  321.6 13.9 %fusion.11 = bf16[800,512]{1,0:T(8,128)(2,1)} fusion(bf16[7200,800]{1,0:T(8,128)(2,1)} %reshape.103, bf16[14400,512]{1,0:T(8,128)(2,1)} %constant_dynamic-update-slice_fusion, s32[]{:T(128)S(6)} %select_n.154), kind=kOutput, calls=%fused_computation.33 | convolution fusion | flops 5898649600 | bytes 21094404 | tf_op jit(solution)/shard_map/dot_general | solution.py:52
  (19 shorter events, 0.1 us)
Async XLA Ops:
  8.0 28.2 %copy-start = (bf16[64,256]{1,0:T(8,128)(2,1)S(1)}, bf16[64,256]{1,0:T(8,128)(2,1)}, u32[]{:S(2)}) copy-start(bf16[64,256]{1,0:T(8,128)(2,1)} %param.7) | copy-start | bytes 98308
  8.0 296.9 %reduce-scatter.2.cloned.1.call-start = ((), (), s32[]{:S(2)}) async-start(), calls=%async_computation.2 | async-start | bytes 9338880 | tf_op jit(solution)/shard_map/reduce_scatter | solution.py:59
  40.4 1.5 copy-start.1
  40.4 116.3 %copy-start.3 = (s32[100]{0:T(128)S(1)}, s32[100]{0:T(128)}, u32[]{:S(2)}) copy-start(s32[100]{0:T(128)} %param.8) | copy-start | bytes 1204
  40.4 116.4 %copy-start.2 = (s32[900]{0:T(1024)S(1)}, s32[900]{0:T(1024)}, u32[]{:S(2)}) copy-start(s32[900]{0:T(1024)} %param.9) | copy-start | bytes 10804
  40.4 269.1 %all-gather.3.cloned.1.call-start = ((), (), s32[]{:S(2)}) async-start(), calls=%async_computation.3 | async-start | bytes 14579712 | tf_op jit(solution)/shard_map/all_gather | solution.py:53
  41.9 79.9 %collective-permute-start = (bf16[1800,512]{1,0:T(8,128)(2,1)S(1)}, bf16[1800,512]{1,0:T(8,128)(2,1)}, u32[]{:S(2)}, u32[]{:S(2)}) collective-permute-start(bf16[1800,512]{1,0:T(8,128)(2,1)S(1)} %copy-done.1), channel_id=1, source_target_pairs={{0,8},{8,16},{16,24},{24,0},{1,9},{9,17},{17,25},{25,1},{2,10},{10... | collective-permute-start | bytes 5529608 | tf_op jit(solution)/shard_map/ppermute | solution.py:20
  121.8 116.2 %collective-permute-start.1 = (bf16[1800,512]{1,0:T(8,128)(2,1)}, bf16[1800,512]{1,0:T(8,128)(2,1)}, u32[]{:S(2)}, u32[]{:S(2)}) collective-permute-start(bf16[1800,512]{1,0:T(8,128)(2,1)} %collective-permute-done), channel_id=1, source_target_pairs={{0,8},{8,16},{16,24},{24,0},{1,9},{9,17},{17,25},{25,1},{2,10},{10... | collective-permute-start | bytes 5529608 | tf_op jit(solution)/shard_map/ppermute | solution.py:20
  238.0 46.9 %collective-permute-start.2 = (bf16[1800,512]{1,0:T(8,128)(2,1)}, bf16[1800,512]{1,0:T(8,128)(2,1)}, u32[]{:S(2)}, u32[]{:S(2)}) collective-permute-start(bf16[1800,512]{1,0:T(8,128)(2,1)} %collective-permute-done.1), channel_id=1, source_target_pairs={{0,8},{8,16},{16,24},{24,0},{1,9},{9,17},{17,25},{25,1},{2,10},{10... | collective-permute-start | bytes 5529608 | tf_op jit(solution)/shard_map/ppermute | solution.py:20
Sparse Core Ops, SparseCore 0:
  40.5 209.2 reduce-scatter.1
Sparse Core Ops, SparseCore 1:
  42.8 73.7 all-gather.2
